TPU v7x, 256 devices: a whole 4x4x8 slice. The times are simulated.
256 devices in a mesh: gx: 8 (over y, core), gy: 32 (over z, x).
Axes of the slice: x: 4, y: 4, z: 8, core: 2. Of those that a mesh axis runs over, the one named last changes fastest.
Arguments:
- state_mean: float32 [2, 512, 1024], P(None, 'gy', 'gx'), may hold values from -6 to 6
- state_spread: bfloat16 [2, 512, 1024, 128], P(None, 'gy', 'gx'), may hold values from -6 to 6
- obs_value: float32 [2, 8, 32, 4], replicated, may hold values from -8 to 8
- obs_var: float32 [2, 8, 32, 4], replicated, may hold values from 0.25 to 4
- obs_col: int32 [2, 8, 32, 4], replicated, may hold values from 0 to 127
- obs_row: int32 [2, 8, 32, 4], replicated, may hold values from 0 to 15
- obs_level: int32 [2, 8, 32, 4], replicated, may hold values from 0 to 1
Outputs:
- analysis_mean: float32 [2, 512, 1024], P(None, 'gy', 'gx')
- analysis_spread: bfloat16 [2, 512, 1024, 128], P(None, 'gy', 'gx')
All inputs are finite; a program needn't handle non-finite values.
Results may differ from a plain program's by a relative error of at most 0.011.
Values may be sent and summed in bfloat16 or wider, within the bound.
A program may use at most 64 MiB of HBM per device.

v0:
```python
import jax
import jax.numpy as jnp
from jax import lax
from jax.sharding import PartitionSpec as P

PRECISE = lax.Precision.HIGHEST


def taper(dist_sq, radius):
    ratio = jnp.sqrt(dist_sq) / radius
    ratio_safe = jnp.maximum(ratio, 1.0)
    inner_part = (((-0.25 * ratio + 0.5) * ratio + 0.625) * ratio - 5.0 / 3.0) * ratio * ratio + 1.0
    outer_part = (
        ((((ratio / 12.0 - 0.5) * ratio + 0.625) * ratio + 5.0 / 3.0) * ratio - 5.0) * ratio
        + 4.0
        - 2.0 / (3.0 * ratio_safe)
    )
    return jnp.where(ratio <= 1.0, inner_part, jnp.where(ratio < 2.0, outer_part, 0.0))


def add_panel(totals, panel, obs_x, obs_y, spread_rows, row_y, col_x, radius):
    panel_zb, panel_qb, panel_eb = panel
    members = spread_rows.shape[2]
    delta_x = (col_x[:, None] - obs_x[None, :]).astype(jnp.float32)
    delta_y = (row_y[:, None] - obs_y[None, :]).astype(jnp.float32)
    taper_vals = taper(delta_x * delta_x + delta_y * delta_y, radius)

    def per_level(operands):
        spread_lev, mean_inc, spread_inc = operands
        covariance = jnp.dot(spread_lev, panel_zb.T, preferred_element_type=jnp.float32) / (
            members - 1.0
        )
        gain_bf = (taper_vals * covariance).astype(jnp.bfloat16)
        mean_inc = mean_inc + jnp.dot(gain_bf, panel_eb, preferred_element_type=jnp.float32)
        spread_inc = spread_inc + jnp.dot(gain_bf, panel_qb, preferred_element_type=jnp.float32)
        return (mean_inc, spread_inc)

    return lax.map(per_level, (spread_rows, totals[0], totals[1]))


def body(state_mean, state_spread, obs_value, obs_var, obs_col, obs_row, obs_level):
    levels, rows_y, cols_x, members = state_spread.shape
    count_x = lax.axis_size("gx")
    count_y = lax.axis_size("gy")
    radius = count_x * cols_x // 2
    at_x = lax.axis_index("gx")
    at_y = lax.axis_index("gy")
    blocks = obs_value.shape[0]
    root_dof = jnp.sqrt(jnp.float32(members - 1))
    identity = jnp.eye(members, dtype=jnp.float32)
    cell_count = rows_y * cols_x
    cell_ids = jnp.arange(cell_count, dtype=jnp.int32)
    row_y = at_y * rows_y + cell_ids // cols_x
    col_x = at_x * cols_x + cell_ids % cols_x
    mean_now = state_mean.reshape(levels, cell_count)
    spread = state_spread.reshape(levels, cell_count, members)
    for block_idx in range(blocks):
        loc_x = obs_col[block_idx][at_x, at_y]
        loc_y = obs_row[block_idx][at_x, at_y]
        loc_lev = obs_level[block_idx][at_x, at_y]
        flat_cell = loc_y * cols_x + loc_x
        prior_obs = mean_now[loc_lev, flat_cell]
        panel_z = spread[loc_lev, flat_cell, :].astype(jnp.float32)
        obs_sd = jnp.sqrt(obs_var[block_idx][at_x, at_y])
        weighted = panel_z / (obs_sd[:, None] * root_dof)
        innov_norm = (obs_value[block_idx][at_x, at_y] - prior_obs) / obs_sd
        zeros_init = (
            jnp.zeros((levels, cell_count), jnp.float32),
            jnp.zeros((levels, cell_count, members), jnp.float32),
        )
        all_x = (
            jnp.arange(count_x, dtype=jnp.int32)[:, None, None] * cols_x + obs_col[block_idx]
        ).reshape(-1)
        all_y = (
            jnp.arange(count_y, dtype=jnp.int32)[None, :, None] * rows_y + obs_row[block_idx]
        ).reshape(-1)
        gram_term = jnp.dot(weighted.T, weighted, precision=PRECISE)
        proj_term = jnp.dot(weighted.T, innov_norm, precision=PRECISE)
        gram_all, proj_all = lax.psum((gram_term, proj_term), ("gx", "gy"))
        factor = jnp.linalg.cholesky(identity + gram_all)
        ens_weights = jax.scipy.linalg.cho_solve((factor, True), proj_all)
        panel_e = (innov_norm - jnp.dot(weighted, ens_weights, precision=PRECISE)) / obs_sd
        solved = jax.scipy.linalg.cho_solve((factor, True), weighted.T)
        panel_q = (root_dof / obs_sd)[:, None] * solved.T
        panel_zb = panel_z.astype(jnp.bfloat16)
        panel_qb = panel_q.astype(jnp.bfloat16)
        panel_eb = panel_e.astype(jnp.bfloat16)
        totals = add_panel(
            zeros_init,
            (
                lax.all_gather(panel_zb, ("gx", "gy"), axis=0, tiled=True),
                lax.all_gather(panel_qb, ("gx", "gy"), axis=0, tiled=True),
                lax.all_gather(panel_eb, ("gx", "gy"), axis=0, tiled=True),
            ),
            all_x,
            all_y,
            spread,
            row_y,
            col_x,
            radius,
        )
        mean_now = mean_now + totals[0]
        spread = (spread.astype(jnp.float32) - 0.5 * totals[1]).astype(jnp.bfloat16)
    return (
        mean_now.reshape(levels, rows_y, cols_x),
        spread.reshape(levels, rows_y, cols_x, members),
    )


def solution(mesh):
    return jax.shard_map(
        body,
        mesh=mesh,
        in_specs=(P(None, "gy", "gx"), P(None, "gy", "gx", None), P(), P(), P(), P(), P()),
        out_specs=(P(None, "gy", "gx"), P(None, "gy", "gx", None)),
        check_vma=False,
    )
```

profile of v0, /device:TPU:1, one launch (start us, length us, event | category | flops | bytes accessed | tf_op | source)
XLA Modules:
  0.0 903.8 jit_solution(16388274281650954638)
XLA Ops:
  7.2 0.7 fusion.89
  8.0 0.7 fusion.90
  8.7 0.7 fusion.88
  9.4 0.7 fusion.87
  10.6 1.4 gather_fusion
  12.0 1.0 fusion.84
  13.3 0.7 copy.38
  14.0 0.6 gather_fusion.1
  14.7 0.7 fusion.86
  15.4 66.7 %all-gather = bf16[256,4,128]{2,1,0:T(4,128)(2,1)S(1)} all-gather(bf16[1,4,128]{2,1,0:T(4,128)(2,1)S(1)} %bitcast.216), channel_id=1, replica_groups=mesh['gx'=8,'gy'=32] {'gx','gy'}, dimensions={0}, use_global_device_ids=true | all-gather | bytes 263168 | tf_op jit(solution)/shard_map/all_gather | solution.py:91
  83.5 0.7 multiply_reduce_fusion
  86.1 0.7 fusion.62
  86.8 75.3 %psum.29 = f32[128]{0:T(128)S(1)} all-reduce(f32[128]{0:T(128)S(1)} %convolution_bitcast_fusion.9), channel_id=1, replica_groups=mesh['gx'=8,'gy'=32] {'gx','gy'}, use_global_device_ids=true, to_apply=%region_3.5 | all-reduce | flops 128 | bytes 1024 | tf_op jit(solution)/shard_map/psum | solution.py:79
  162.1 98.1 %all-reduce.5.cloned.1.call-done = f32[128,128]{0,1:T(8,128)} async-done(((f32[128,128]{0,1:T(8,128)}), f32[128,128]{0,1:T(8,128)}) %all-reduce.5.cloned.1.call-update) | async-done | bytes 65552 | tf_op jit(solution)/shard_map/psum | solution.py:79
  260.2 0.9 convert_add_fusion.1
  261.1 0.9 fusion.45
  262.0 11.7 %cholesky.44 = f32[128,128]{1,0:T(8,128)S(1)} custom-call(f32[128,128]{1,0:T(8,128)S(1)} %fusion.45), custom_call_target="Cholesky" | custom-call | tf_op jit(solution)/shard_map/jit(cholesky)/cholesky | solution.py:80
  274.4 0.7 fusion.32
  275.1 9.8 %custom-call.22 = f32[1,128,128]{1,2,0:T(8,128)S(1)} custom-call(f32[1,128,128]{2,1,0:T(8,128)S(1)} %fusion.32), custom_call_target="InvertDiagBlocksLowerTriangular" | custom-call | tf_op jit(solution)/shard_map/jit(_cho_solve)/triangular_solve | solution.py:81
  285.3 59.9 %all-gather.1 = bf16[256,4,128]{2,1,0:T(4,128)(2,1)S(1)} all-gather(bf16[1,4,128]{2,1,0:T(4,128)(2,1)S(1)} %fusion.25), channel_id=1, replica_groups=mesh['gx'=8,'gy'=32] {'gx','gy'}, dimensions={0}, use_global_device_ids=true | all-gather | bytes 263168 | tf_op jit(solution)/shard_map/all_gather | solution.py:92
  346.0 76.5 %all-reduce = bf16[1024]{0:T(1024)(128)(2,1)S(1)} all-reduce(bf16[1024]{0:T(1024)(128)(2,1)S(1)} %dynamic-update-slice.2), channel_id=1, replica_groups=mesh['gx'=8,'gy'=32] {'gx','gy'}, use_global_device_ids=true, to_apply=%add | all-reduce | flops 1024 | bytes 4096
  422.7 34.6 %while.26 = (s32[]{:T(128)}, f32[2,2048]{1,0:T(2,128)S(1)}, f32[2,2048,128]{2,1,0:T(8,128)S(1)}, bf16[2,2048,128]{2,1,0:T(8,128)(2,1)}, bf16[1024,128]{1,0:T(8,1...) while((s32[]{:T(128)}, f32[2,2048]{1,0:T(2,128)S(1)}, ...), condition=%wide.region_5.9_spmd.clone, body=%wide.region_4.8_spmd.clone.sunk | while | flops 1157627904 | bytes 14736005 | solution.py:38
  422.7 14.7 %fusion.135 = bf16[2048,1024]{1,0:T(8,128)(2,1)S(1)} fusion(bf16[1024,128]{1,0:T(8,128)(2,1)S(1)} %get-tuple-element.386, s32[1024]{0:T(1024)S(1)} %get-tuple-element.391, s32[2048]{0:T(1024)S(1)} %get-tuple-element.392, s32[1024]{0:T(1024)S(1)} %get-tuple-element.389, s32[2048]{0:T(1024)S(1)} %get-tuple-element.390, ...), kind=kOutput, calls=%fused_computation.10.clone.1 | convolution fusion | flops 616562688 | bytes 5005824 | tf_op jit(solution)/shard_map/while/body/eval_jaxpr/dot_general | solution.py:30
  437.5 1.3 fusion.137
  438.7 1.2 fusion.136
  440.0 14.7 %fusion.135 = bf16[2048,1024]{1,0:T(8,128)(2,1)S(1)} fusion(bf16[1024,128]{1,0:T(8,128)(2,1)S(1)} %get-tuple-element.386, s32[1024]{0:T(1024)S(1)} %get-tuple-element.391, s32[2048]{0:T(1024)S(1)} %get-tuple-element.392, s32[1024]{0:T(1024)S(1)} %get-tuple-element.389, s32[2048]{0:T(1024)S(1)} %get-tuple-element.390, ...), kind=kOutput, calls=%fused_computation.10.clone.1 | convolution fusion | flops 616562688 | bytes 5005824 | tf_op jit(solution)/shard_map/while/body/eval_jaxpr/dot_general | solution.py:30
  454.7 1.3 fusion.137
  456.0 1.2 fusion.136
  457.4 1.5 subtract_convert_fusion.1
  459.5 1.0 fusion.85
  461.2 62.8 %all-gather.2 = bf16[256,4,128]{2,1,0:T(4,128)(2,1)} all-gather(bf16[1,4,128]{2,1,0:T(4,128)(2,1)S(1)} %bitcast.217), channel_id=1, replica_groups=mesh['gx'=8,'gy'=32] {'gx','gy'}, dimensions={0}, use_global_device_ids=true | all-gather | bytes 263168 | tf_op jit(solution)/shard_map/all_gather | solution.py:91
  524.2 77.2 %psum.31 = f32[128]{0:T(128)S(1)} all-reduce(f32[128]{0:T(128)S(1)} %convolution_bitcast_fusion.5), channel_id=1, replica_groups=mesh['gx'=8,'gy'=32] {'gx','gy'}, use_global_device_ids=true, to_apply=%region_7.11 | all-reduce | flops 128 | bytes 1024 | tf_op jit(solution)/shard_map/psum | solution.py:79
  601.5 95.7 %all-reduce.7.cloned.1.call-done = f32[128,128]{0,1:T(8,128)} async-done(((f32[128,128]{0,1:T(8,128)}), f32[128,128]{0,1:T(8,128)}) %all-reduce.7.cloned.1.call-update) | async-done | bytes 65552 | tf_op jit(solution)/shard_map/psum | solution.py:79
  697.2 0.9 convert_add_fusion
  698.1 0.9 fusion.39
  699.0 11.7 %cholesky.55 = f32[128,128]{1,0:T(8,128)S(1)} custom-call(f32[128,128]{1,0:T(8,128)S(1)} %fusion.39), custom_call_target="Cholesky" | custom-call | tf_op jit(solution)/shard_map/jit(cholesky)/cholesky | solution.py:80
  711.4 0.7 fusion.33
  712.0 9.8 %custom-call.24 = f32[1,128,128]{1,2,0:T(8,128)S(1)} custom-call(f32[1,128,128]{2,1,0:T(8,128)S(1)} %fusion.33), custom_call_target="InvertDiagBlocksLowerTriangular" | custom-call | tf_op jit(solution)/shard_map/jit(_cho_solve)/triangular_solve | solution.py:81
  722.2 59.9 %all-gather.3 = bf16[256,4,128]{2,1,0:T(4,128)(2,1)S(1)} all-gather(bf16[1,4,128]{2,1,0:T(4,128)(2,1)S(1)} %fusion.24), channel_id=1, replica_groups=mesh['gx'=8,'gy'=32] {'gx','gy'}, dimensions={0}, use_global_device_ids=true | all-gather | bytes 263168 | tf_op jit(solution)/shard_map/all_gather | solution.py:92
  783.0 76.6 %all-reduce.1 = bf16[1024]{0:T(1024)(128)(2,1)S(1)} all-reduce(bf16[1024]{0:T(1024)(128)(2,1)S(1)} %dynamic-update-slice.3), channel_id=1, replica_groups=mesh['gx'=8,'gy'=32] {'gx','gy'}, use_global_device_ids=true, to_apply=%add.1 | all-reduce | flops 1024 | bytes 4096
  859.8 35.3 %while.27 = (s32[]{:T(128)}, f32[2,2048]{1,0:T(2,128)S(1)}, f32[2,2048,128]{2,1,0:T(8,128)S(1)}, bf16[2,2048,128]{2,1,0:T(8,128)(2,1)S(1)}, bf16[1024,128]{1,0:T...) while((s32[]{:T(128)}, f32[2,2048]{1,0:T(2,128)S(1)}, ...), condition=%wide.region_9.13_spmd.clone, body=%wide.region_8.12_spmd.clone.sunk | while | flops 1157627904 | bytes 14735497 | solution.py:38
  859.8 15.1 %fusion.144 = bf16[2048,1024]{1,0:T(8,128)(2,1)S(1)} fusion(bf16[1024,128]{1,0:T(8,128)(2,1)} %get-tuple-element.425, s32[1024]{0:T(1024)S(1)} %get-tuple-element.430, s32[2048]{0:T(1024)S(1)} %get-tuple-element.431, s32[1024]{0:T(1024)S(1)} %get-tuple-element.428, s32[2048]{0:T(1024)S(1)} %get-tuple-element.429, ...), kind=kOutput, calls=%fused_computation.24.clone.1 | convolution fusion | flops 616562688 | bytes 5005316 | tf_op jit(solution)/shard_map/while/body/eval_jaxpr/dot_general | solution.py:30
  874.9 1.3 fusion.146
  876.2 1.2 fusion.145
  877.5 15.1 %fusion.144 = bf16[2048,1024]{1,0:T(8,128)(2,1)S(1)} fusion(bf16[1024,128]{1,0:T(8,128)(2,1)} %get-tuple-element.425, s32[1024]{0:T(1024)S(1)} %get-tuple-element.430, s32[2048]{0:T(1024)S(1)} %get-tuple-element.431, s32[1024]{0:T(1024)S(1)} %get-tuple-element.428, s32[2048]{0:T(1024)S(1)} %get-tuple-element.429, ...), kind=kOutput, calls=%fused_computation.24.clone.1 | convolution fusion | flops 616562688 | bytes 5005316 | tf_op jit(solution)/shard_map/while/body/eval_jaxpr/dot_general | solution.py:30
  892.5 1.3 fusion.146
  893.8 1.2 fusion.145
  895.1 1.2 subtract_convert_fusion
  (88 shorter events, 10.7 us)
Async XLA Ops:
  7.2 253.0 %all-reduce.5.cloned.1.call-start = ((), (), s32[]{:S(2)}) async-start(), calls=%async_computation | async-start | bytes 131072 | tf_op jit(solution)/shard_map/psum | solution.py:79
  13.0 684.2 %all-reduce.7.cloned.1.call-start = ((), (), s32[]{:S(2)}) async-start(), calls=%async_computation.1 | async-start | bytes 131072 | tf_op jit(solution)/shard_map/psum | solution.py:79
  84.2 338.5 %copy-start.9 = (f32[4]{0:T(128)}, f32[4]{0:T(128)S(1)}, u32[]{:S(2)}) copy-start(f32[4]{0:T(128)S(1)} %get-tuple-element.152) | copy-start | bytes 52
  457.3 1.6 copy-start.3
  457.3 2.2 copy-start.7
  457.3 3.2 copy-start.2
  457.3 66.7 %copy-start.8 = (f32[4]{0:T(128)S(1)}, f32[4]{0:T(128)}, u32[]{:S(2)}) copy-start(f32[4]{0:T(128)} %fusion.62) | copy-start | bytes 52
  457.4 66.7 %copy-start.10 = (f32[4]{0:T(128)S(1)}, f32[4]{0:T(128)}, u32[]{:S(2)}) copy-start(f32[4]{0:T(128)} %copy-done.9) | copy-start | bytes 52
  457.4 264.7 %copy-start.6 = (f32[4]{0:T(128)S(1)}, f32[4]{0:T(128)}, u32[]{:S(2)}) copy-start(f32[4]{0:T(128)} %get-tuple-element.151) | copy-start | bytes 52
  457.4 402.4 %copy-start.4 = (s32[1024]{0:T(1024)S(1)}, s32[1024]{0:T(1024)}, u32[]{:S(2)}) copy-start(s32[1024]{0:T(1024)} %get-tuple-element.404) | copy-start | bytes 12292
  457.4 402.4 %copy-start.5 = (s32[1024]{0:T(1024)S(1)}, s32[1024]{0:T(1024)}, u32[]{:S(2)}) copy-start(s32[1024]{0:T(1024)} %get-tuple-element.402) | copy-start | bytes 12292
  460.6 399.2 %copy-start = (f32[2,2048]{1,0:T(2,128)}, f32[2,2048]{1,0:T(2,128)S(1)}, u32[]{:S(2)}) copy-start(f32[2,2048]{1,0:T(2,128)S(1)} %fusion.83) | copy-start | bytes 49156
  895.1 1.3 copy-start.1
Sparse Core Ops, SparseCore 0:
  14.1 246.0 all-reduce.4
  460.6 236.4 all-reduce.6
where the time goes:
time: 906 us; the launch traced here: 904 us
  blocking collectives  555 us (61%)
  waiting for transfers between devices  194 us (21%)
  matrix products  73.8 us (8%)
  other arithmetic  54.9 us (6%)
  between operations  14.4 us (2%)
  local copies, waits for them, and re-layouts  11.7 us (1%)
    psum x2, waiting for transfers between devices, body(): gram_all, proj_all = lax.psum((gram_term, proj_term), ('gx', 'gy'))  194 us
    unnamed x2, blocking collectives  153 us
    psum x2, blocking collectives, body(): gram_all, proj_all = lax.psum((gram_term, proj_term), ('gx', 'gy'))  153 us
    all_gather x2, blocking collectives, body(): lax.all_gather(panel_zb, ('gx', 'gy'), axis=0, tiled=True)  130 us
    all_gather x2, blocking collectives, body(): lax.all_gather(panel_qb, ('gx', 'gy'), axis=0, tiled=True)  120 us
    dot_general x4, matrix products, per_level(): jnp.dot(spread_lev, panel_zb.T, preferred_element_type=jnp.float32)  59.5 us
    another operation x6, other arithmetic, body(): factor = jnp.linalg.cholesky(identity + gram_all)  24.8 us
    another operation x4, other arithmetic, body(): ens_weights = jax.scipy.linalg.cho_solve((factor, True), proj_all)  20.9 us
  transfers between devices with their start and end apart: 2, of which 2 were waited for; matrix products, arithmetic and copies ran while one was open for 1% of the time, Pallas kernels for 0%

commit v1 on v0

--- a/solution.py
+++ b/solution.py
@@ -76,7 +76,7 @@
         ).reshape(-1)
         gram_term = jnp.dot(weighted.T, weighted, precision=PRECISE)
         proj_term = jnp.dot(weighted.T, innov_norm, precision=PRECISE)
-        gram_all, proj_all = lax.psum((gram_term, proj_term), ("gx", "gy"))
+        gram_all, proj_all = lax.psum(lax.psum((gram_term, proj_term), "gy"), "gx")
         factor = jnp.linalg.cholesky(identity + gram_all)
         ens_weights = jax.scipy.linalg.cho_solve((factor, True), proj_all)
         panel_e = (innov_norm - jnp.dot(weighted, ens_weights, precision=PRECISE)) / obs_sd

time: 906 us -> 874 us (0.965)
  waiting for transfers between devices: 194 us -> 137 us
  blocking collectives: 555 us -> 580 us
    psum x2 -> x4, waiting for transfers between devices: 194 us -> 137 us  [body(): gram_all, proj_all = lax.psum(lax.psum((gram_term, proj_term), 'gy'), 'gx')]
    psum x2 -> x4, blocking collectives: 153 us -> 179 us  [body(): gram_all, proj_all = lax.psum(lax.psum((gram_term, proj_term), 'gy'), 'gx')]
  transfers between devices with their start and end apart: 2 -> 4, of which waited for: 2 -> 2; matrix products, arithmetic and copies ran while one was open for 1% -> 1% of each run, Pallas kernels for 0% -> 0%
where the time goes in v1:
time: 874 us; the launch traced here: 872 us
  blocking collectives  580 us (66%)
  waiting for transfers between devices  137 us (16%)
  matrix products  73.7 us (8%)
  other arithmetic  55 us (6%)
  between operations  14.1 us (2%)
  local copies, waits for them, and re-layouts  11.8 us (1%)
    psum x4, blocking collectives, body(): gram_all, proj_all = lax.psum(lax.psum((gram_term, proj_term), 'gy'), 'gx')  179 us
    unnamed x2, blocking collectives  155 us
    psum x4, waiting for transfers between devices, body(): gram_all, proj_all = lax.psum(lax.psum((gram_term, proj_term), 'gy'), 'gx')  137 us
    all_gather x2, blocking collectives, body(): lax.all_gather(panel_zb, ('gx', 'gy'), axis=0, tiled=True)  130 us
    all_gather x2, blocking collectives, body(): lax.all_gather(panel_qb, ('gx', 'gy'), axis=0, tiled=True)  116 us
    dot_general x4, matrix products, per_level(): jnp.dot(spread_lev, panel_zb.T, preferred_element_type=jnp.float32)  59.5 us
    another operation x6, other arithmetic, body(): factor = jnp.linalg.cholesky(identity + gram_all)  24.8 us
    another operation x4, other arithmetic, body(): ens_weights = jax.scipy.linalg.cho_solve((factor, True), proj_all)  20.9 us
  transfers between devices with their start and end apart: 4, of which 2 were waited for; matrix products, arithmetic and copies ran while one was open for 1% of the time, Pallas kernels for 0%

profile of v1, /device:TPU:1, one launch (start us, length us, event | category | flops | bytes accessed | tf_op | source)
XLA Modules:
  0.0 872.4 jit_solution(8183141982680188306)
XLA Ops:
  7.2 0.7 fusion.89
  8.0 0.7 fusion.90
  8.7 0.7 fusion.88
  9.4 0.7 fusion.87
  10.6 1.4 gather_fusion
  12.0 1.0 fusion.84
  13.3 0.7 copy.38
  14.7 0.7 fusion.86
  15.4 66.7 %all-gather = bf16[256,4,128]{2,1,0:T(4,128)(2,1)S(1)} all-gather(bf16[1,4,128]{2,1,0:T(4,128)(2,1)S(1)} %bitcast.216), channel_id=1, replica_groups=mesh['gx'=8,'gy'=32] {'gx','gy'}, dimensions={0}, use_global_device_ids=true | all-gather | bytes 263168 | tf_op jit(solution)/shard_map/all_gather | solution.py:91
  83.5 0.8 multiply_reduce_fusion
  86.2 67.9 %all-reduce.7.cloned.1.call-done = f32[128,128]{0,1:T(8,128)} async-done(((f32[128,128]{0,1:T(8,128)}), f32[128,128]{0,1:T(8,128)}) %all-reduce.7.cloned.1.call-update) | async-done | bytes 65552 | tf_op jit(solution)/shard_map/psum | solution.py:79
  154.2 0.8 fusion.62
  154.9 58.8 %psum.58 = f32[128]{0:T(128)S(1)} all-reduce(f32[128]{0:T(128)S(1)} %convolution_bitcast_fusion.9), channel_id=1, replica_groups=mesh['gx'=8,'gy'=32] {'gy'}, use_global_device_ids=true, to_apply=%region_4.6 | all-reduce | flops 128 | bytes 1024 | tf_op jit(solution)/shard_map/psum | solution.py:79
  213.8 30.7 %psum.59 = f32[128]{0:T(128)S(1)} all-reduce(f32[128]{0:T(128)S(1)} %psum.58), channel_id=1, replica_groups=mesh['gx'=8,'gy'=32] {'gx'}, use_global_device_ids=true, to_apply=%region_5.7 | all-reduce | flops 128 | bytes 1024 | tf_op jit(solution)/shard_map/psum | solution.py:79
  244.5 0.9 convert_add_fusion.1
  245.5 0.9 fusion.45
  246.3 11.7 %cholesky.44 = f32[128,128]{1,0:T(8,128)S(1)} custom-call(f32[128,128]{1,0:T(8,128)S(1)} %fusion.45), custom_call_target="Cholesky" | custom-call | tf_op jit(solution)/shard_map/jit(cholesky)/cholesky | solution.py:80
  258.7 0.7 fusion.32
  259.4 9.8 %custom-call.22 = f32[1,128,128]{1,2,0:T(8,128)S(1)} custom-call(f32[1,128,128]{2,1,0:T(8,128)S(1)} %fusion.32), custom_call_target="InvertDiagBlocksLowerTriangular" | custom-call | tf_op jit(solution)/shard_map/jit(_cho_solve)/triangular_solve | solution.py:81
  269.6 57.9 %all-gather.1 = bf16[256,4,128]{2,1,0:T(4,128)(2,1)S(1)} all-gather(bf16[1,4,128]{2,1,0:T(4,128)(2,1)S(1)} %fusion.25), channel_id=1, replica_groups=mesh['gx'=8,'gy'=32] {'gx','gy'}, dimensions={0}, use_global_device_ids=true | all-gather | bytes 263168 | tf_op jit(solution)/shard_map/all_gather | solution.py:92
  328.3 77.4 %all-reduce = bf16[1024]{0:T(1024)(128)(2,1)S(1)} all-reduce(bf16[1024]{0:T(1024)(128)(2,1)S(1)} %dynamic-update-slice.2), channel_id=1, replica_groups=mesh['gx'=8,'gy'=32] {'gx','gy'}, use_global_device_ids=true, to_apply=%add | all-reduce | flops 1024 | bytes 4096
  405.9 34.6 %while.26 = (s32[]{:T(128)}, f32[2,2048]{1,0:T(2,128)S(1)}, f32[2,2048,128]{2,1,0:T(8,128)S(1)}, bf16[2,2048,128]{2,1,0:T(8,128)(2,1)}, bf16[1024,128]{1,0:T(8,1...) while((s32[]{:T(128)}, f32[2,2048]{1,0:T(2,128)S(1)}, ...), condition=%wide.region_7.11_spmd.clone, body=%wide.region_6.10_spmd.clone.sunk | while | flops 1157627904 | bytes 14736005 | solution.py:38
  405.9 14.7 %fusion.135 = bf16[2048,1024]{1,0:T(8,128)(2,1)S(1)} fusion(bf16[1024,128]{1,0:T(8,128)(2,1)S(1)} %get-tuple-element.386, s32[1024]{0:T(1024)S(1)} %get-tuple-element.391, s32[2048]{0:T(1024)S(1)} %get-tuple-element.392, s32[1024]{0:T(1024)S(1)} %get-tuple-element.389, s32[2048]{0:T(1024)S(1)} %get-tuple-element.390, ...), kind=kOutput, calls=%fused_computation.10.clone.1 | convolution fusion | flops 616562688 | bytes 5005824 | tf_op jit(solution)/shard_map/while/body/eval_jaxpr/dot_general | solution.py:30
  420.6 1.3 fusion.137
  421.9 1.2 fusion.136
  423.2 14.7 %fusion.135 = bf16[2048,1024]{1,0:T(8,128)(2,1)S(1)} fusion(bf16[1024,128]{1,0:T(8,128)(2,1)S(1)} %get-tuple-element.386, s32[1024]{0:T(1024)S(1)} %get-tuple-element.391, s32[2048]{0:T(1024)S(1)} %get-tuple-element.392, s32[1024]{0:T(1024)S(1)} %get-tuple-element.389, s32[2048]{0:T(1024)S(1)} %get-tuple-element.390, ...), kind=kOutput, calls=%fused_computation.10.clone.1 | convolution fusion | flops 616562688 | bytes 5005824 | tf_op jit(solution)/shard_map/while/body/eval_jaxpr/dot_general | solution.py:30
  437.9 1.3 fusion.137
  439.2 1.2 fusion.136
  440.5 1.5 subtract_convert_fusion.1
  442.6 1.0 fusion.85
  444.4 63.2 %all-gather.2 = bf16[256,4,128]{2,1,0:T(4,128)(2,1)} all-gather(bf16[1,4,128]{2,1,0:T(4,128)(2,1)S(1)} %bitcast.217), channel_id=1, replica_groups=mesh['gx'=8,'gy'=32] {'gx','gy'}, dimensions={0}, use_global_device_ids=true | all-gather | bytes 263168 | tf_op jit(solution)/shard_map/all_gather | solution.py:91
  507.6 69.5 %all-reduce.11.cloned.1.call-done = f32[128,128]{0,1:T(8,128)} async-done(((f32[128,128]{0,1:T(8,128)}), f32[128,128]{0,1:T(8,128)}) %all-reduce.11.cloned.1.call-update) | async-done | bytes 65552 | tf_op jit(solution)/shard_map/psum | solution.py:79
  577.3 58.9 %psum.62 = f32[128]{0:T(128)S(1)} all-reduce(f32[128]{0:T(128)S(1)} %convolution_bitcast_fusion.5), channel_id=1, replica_groups=mesh['gx'=8,'gy'=32] {'gy'}, use_global_device_ids=true, to_apply=%region_10.14 | all-reduce | flops 128 | bytes 1024 | tf_op jit(solution)/shard_map/psum | solution.py:79
  636.2 30.9 %psum.63 = f32[128]{0:T(128)S(1)} all-reduce(f32[128]{0:T(128)S(1)} %psum.62), channel_id=1, replica_groups=mesh['gx'=8,'gy'=32] {'gx'}, use_global_device_ids=true, to_apply=%region_11.15 | all-reduce | flops 128 | bytes 1024 | tf_op jit(solution)/shard_map/psum | solution.py:79
  667.1 0.9 convert_add_fusion
  668.1 0.9 fusion.39
  669.0 11.7 %cholesky.55 = f32[128,128]{1,0:T(8,128)S(1)} custom-call(f32[128,128]{1,0:T(8,128)S(1)} %fusion.39), custom_call_target="Cholesky" | custom-call | tf_op jit(solution)/shard_map/jit(cholesky)/cholesky | solution.py:80
  682.0 9.8 %custom-call.24 = f32[1,128,128]{1,2,0:T(8,128)S(1)} custom-call(f32[1,128,128]{2,1,0:T(8,128)S(1)} %fusion.33), custom_call_target="InvertDiagBlocksLowerTriangular" | custom-call | tf_op jit(solution)/shard_map/jit(_cho_solve)/triangular_solve | solution.py:81
  692.2 57.9 %all-gather.3 = bf16[256,4,128]{2,1,0:T(4,128)(2,1)S(1)} all-gather(bf16[1,4,128]{2,1,0:T(4,128)(2,1)S(1)} %fusion.24), channel_id=1, replica_groups=mesh['gx'=8,'gy'=32] {'gx','gy'}, dimensions={0}, use_global_device_ids=true | all-gather | bytes 263168 | tf_op jit(solution)/shard_map/all_gather | solution.py:92
  750.9 77.5 %all-reduce.1 = bf16[1024]{0:T(1024)(128)(2,1)S(1)} all-reduce(bf16[1024]{0:T(1024)(128)(2,1)S(1)} %dynamic-update-slice.3), channel_id=1, replica_groups=mesh['gx'=8,'gy'=32] {'gx','gy'}, use_global_device_ids=true, to_apply=%add.1 | all-reduce | flops 1024 | bytes 4096
  828.6 35.3 %while.27 = (s32[]{:T(128)}, f32[2,2048]{1,0:T(2,128)S(1)}, f32[2,2048,128]{2,1,0:T(8,128)S(1)}, bf16[2,2048,128]{2,1,0:T(8,128)(2,1)S(1)}, bf16[1024,128]{1,0:T...) while((s32[]{:T(128)}, f32[2,2048]{1,0:T(2,128)S(1)}, ...), condition=%wide.region_13.17_spmd.clone, body=%wide.region_12.16_spmd.clone.sunk | while | flops 1157627904 | bytes 14735497 | solution.py:38
  828.6 15.1 %fusion.144 = bf16[2048,1024]{1,0:T(8,128)(2,1)S(1)} fusion(bf16[1024,128]{1,0:T(8,128)(2,1)} %get-tuple-element.425, s32[1024]{0:T(1024)S(1)} %get-tuple-element.430, s32[2048]{0:T(1024)S(1)} %get-tuple-element.431, s32[1024]{0:T(1024)S(1)} %get-tuple-element.428, s32[2048]{0:T(1024)S(1)} %get-tuple-element.429, ...), kind=kOutput, calls=%fused_computation.24.clone.1 | convolution fusion | flops 616562688 | bytes 5005316 | tf_op jit(solution)/shard_map/while/body/eval_jaxpr/dot_general | solution.py:30
  843.7 1.3 fusion.146
  845.0 1.2 fusion.145
  846.3 15.1 %fusion.144 = bf16[2048,1024]{1,0:T(8,128)(2,1)S(1)} fusion(bf16[1024,128]{1,0:T(8,128)(2,1)} %get-tuple-element.425, s32[1024]{0:T(1024)S(1)} %get-tuple-element.430, s32[2048]{0:T(1024)S(1)} %get-tuple-element.431, s32[1024]{0:T(1024)S(1)} %get-tuple-element.428, s32[2048]{0:T(1024)S(1)} %get-tuple-element.429, ...), kind=kOutput, calls=%fused_computation.24.clone.1 | convolution fusion | flops 616562688 | bytes 5005316 | tf_op jit(solution)/shard_map/while/body/eval_jaxpr/dot_general | solution.py:30
  861.4 1.3 fusion.146
  862.7 1.2 fusion.145
  864.0 1.2 subtract_convert_fusion
  (96 shorter events, 12.1 us)
Async XLA Ops:
  7.2 146.9 %all-reduce.7.cloned.1.call-start = ((), (), s32[]{:S(2)}) async-start(), calls=%async_computation | async-start | bytes 131072 | tf_op jit(solution)/shard_map/psum | solution.py:79
  13.0 231.5 %all-reduce.9.cloned.1.call-start = ((), (), s32[]{:S(2)}) async-start(), calls=%async_computation.1 | async-start | bytes 131072 | tf_op jit(solution)/shard_map/psum | solution.py:79
  84.3 321.6 %copy-start.9 = (f32[4]{0:T(128)}, f32[4]{0:T(128)S(1)}, u32[]{:S(2)}) copy-start(f32[4]{0:T(128)S(1)} %get-tuple-element.152) | copy-start | bytes 52
  154.1 423.0 %all-reduce.11.cloned.1.call-start = ((), (), s32[]{:S(2)}) async-start(), calls=%async_computation.2 | async-start | bytes 131072 | tf_op jit(solution)/shard_map/psum | solution.py:79
  440.5 1.6 copy-start.3
  440.5 2.2 copy-start.7
  440.5 3.2 copy-start.2
  440.5 136.6 %copy-start.8 = (f32[4]{0:T(128)S(1)}, f32[4]{0:T(128)}, u32[]{:S(2)}) copy-start(f32[4]{0:T(128)} %fusion.62) | copy-start | bytes 52
  440.5 136.6 %copy-start.10 = (f32[4]{0:T(128)S(1)}, f32[4]{0:T(128)}, u32[]{:S(2)}) copy-start(f32[4]{0:T(128)} %copy-done.9) | copy-start | bytes 52
  440.5 251.5 %copy-start.6 = (f32[4]{0:T(128)S(1)}, f32[4]{0:T(128)}, u32[]{:S(2)}) copy-start(f32[4]{0:T(128)} %get-tuple-element.151) | copy-start | bytes 52
  440.5 388.1 %copy-start.4 = (s32[1024]{0:T(1024)S(1)}, s32[1024]{0:T(1024)}, u32[]{:S(2)}) copy-start(s32[1024]{0:T(1024)} %get-tuple-element.404) | copy-start | bytes 12292
  440.5 388.1 %copy-start.5 = (s32[1024]{0:T(1024)S(1)}, s32[1024]{0:T(1024)}, u32[]{:S(2)}) copy-start(s32[1024]{0:T(1024)} %get-tuple-element.402) | copy-start | bytes 12292
  443.7 223.5 %all-reduce.13.cloned.1.call-start = ((), (), s32[]{:S(2)}) async-start(), calls=%async_computation.3 | async-start | bytes 131072 | tf_op jit(solution)/shard_map/psum | solution.py:79
  443.8 384.9 %copy-start = (f32[2,2048]{1,0:T(2,128)}, f32[2,2048]{1,0:T(2,128)S(1)}, u32[]{:S(2)}) copy-start(f32[2,2048]{1,0:T(2,128)S(1)} %fusion.83) | copy-start | bytes 49156
  863.9 1.3 copy-start.1
Sparse Core Ops, SparseCore 0:
  13.1 140.9 all-reduce.6
  156.4 65.5 all-reduce.8
  443.8 133.2 all-reduce.10
  579.3 65.3 all-reduce.12
